TPU v7x, 32 devices: a whole 2x2x4 slice. The times are simulated.
32 devices in a mesh: rep: 4 (over y, x), mp: 8 (over z, core).
Axes of the slice: x: 2, y: 2, z: 4, core: 2. Of those that a mesh axis runs over, the one named last changes fastest.
Arguments:
- acts: bfloat16 [1024, 64, 256], P('rep', 'mp'), may hold values from -40 to 40, as said below
- refresh: int32 [64], P(('mp', 'rep')), may hold values from 0 to 8, as said below
- damping: float32 [64], P(('mp', 'rep')), may hold values from 0.2 to 1
- old_inverse: bfloat16 [64, 256, 256], P(('mp', 'rep')), may hold values from -0.375 to 0.375
- grads: bfloat16 [1024, 64, 256], P('rep', 'mp'), may hold values from -6 to 6
Outputs:
- covariance: float32 [64, 256, 256], P(('mp', 'rep'))
- new_inverse: bfloat16 [64, 256, 256], P(('mp', 'rep'))
- precond: bfloat16 [1024, 64, 256], P('rep', 'mp')
Inputs may be any that keep to these rules, and one draw needn't show every extreme that they name: `acts`: entries are bfloat16 values of order one with unequal feature scales. Block g * 8 + 2 * r + q (q = 0 or 1) is the q-th block of group g at replica index r. A block is refreshed only by a group through the same r. For every r, each group refreshes exactly one block through r. Of the two blocks of a group at r, at most one is refreshed by another group, and then the other one by the group itself. In every draw some groups refresh a block of another group.
All inputs are finite; a program needn't handle non-finite values. Where the computation divides by a largest or mean magnitude, that divisor is 1e-20 or more.
Results may differ from a plain program's by a relative error of at most 0.009.
Values may be sent and summed in bfloat16 or wider, within the bound.
A program may use at most 64 MiB of HBM per device.

v0:
```python
import jax
import jax.numpy as jnp
from jax import lax
from jax.sharding import PartitionSpec as P

ITERS = 5


HIGHEST_PRECISION = lax.Precision.HIGHEST


def newton_inverse(gram, damp_value):
    order_size = gram.shape[-1]
    identity = jnp.eye(order_size, dtype=jnp.float32)
    matrix = gram + damp_value * identity
    row_bound = jnp.max(jnp.sum(jnp.abs(matrix), axis=1))
    approx = identity / row_bound
    for iteration in range(ITERS):
        product = jnp.dot(
            matrix, approx, precision=HIGHEST_PRECISION, preferred_element_type=jnp.float32
        )
        approx = jnp.dot(
            approx,
            2.0 * identity - product,
            precision=HIGHEST_PRECISION,
            preferred_element_type=jnp.float32,
        )
    return approx


def local(acts, refresh, damping, old_inverse, grads):
    replicas = lax.axis_size("rep")
    groups = lax.axis_size("mp")
    tokens_all = acts.shape[0] * replicas
    held_blocks = refresh.shape[0]
    covariance = (
        lax.psum_scatter(
            jnp.einsum("tkb,tkc->kbc", acts, acts, preferred_element_type=jnp.float32).astype(
                jnp.bfloat16
            ),
            "rep",
            scatter_dimension=0,
            tiled=True,
        ).astype(jnp.float32)
        / tokens_all
    )
    pieces = []
    for slot_index in range(held_blocks):

        def invert_here(slot_index=slot_index):
            return newton_inverse(covariance[slot_index], damping[slot_index]).astype(jnp.bfloat16)

        def keep_stored(slot_index=slot_index):
            return old_inverse[slot_index]

        pieces.append(lax.cond(refresh[slot_index] != groups, invert_here, keep_stored))
    new_inverse = jnp.stack(pieces)
    precond = jnp.einsum(
        "rkb,kbc->rkc",
        grads,
        lax.all_gather(new_inverse, "rep", axis=0, tiled=True),
        preferred_element_type=jnp.float32,
    ).astype(jnp.bfloat16)
    return (covariance, new_inverse, precond)


def solution(mesh):
    return jax.shard_map(
        local,
        mesh=mesh,
        in_specs=(
            P("rep", "mp", None),
            P(("mp", "rep")),
            P(("mp", "rep")),
            P(("mp", "rep"), None, None),
            P("rep", "mp", None),
        ),
        out_specs=(
            P(("mp", "rep"), None, None),
            P(("mp", "rep"), None, None),
            P("rep", "mp", None),
        ),
        check_vma=False,
    )
```

profile of v0, /device:TPU:0, one launch (start us, length us, event | category | flops | bytes accessed | tf_op | source)
XLA Modules:
  0.0 96.5 jit_solution(9774110282836496823)
XLA Ops:
  7.2 0.0 copy-start
  7.2 0.0 reduce-scatter.2.cloned.1.call-start
  7.2 3.2 %convolution_convert_fusion.3 = bf16[8,256,256]{2,1,0:T(8,128)(2,1)} fusion(bf16[256,8,256]{2,1,0:T(8,128)(2,1)} %param.9), kind=kOutput, calls=%fused_computation.39 | convolution fusion | flops 268959744 | bytes 2097152 | tf_op jit(solution)/shard_map/tkb,tkc->kbc/dot_general | solution.py:38
  10.5 0.0 copy-start.4
  10.5 0.0 copy-start.2
  10.5 0.0 copy-start.3
  10.5 0.0 reduce-scatter.2.cloned.1.call-update
  10.5 0.0 all-gather.2.cloned.1.call-start
  10.5 0.6 copy-done.4
  11.1 0.6 fusion.23
  13.0 29.2 %reduce-scatter.2.cloned.1.call-done = bf16[2,256,256]{2,1,0:T(8,128)(2,1)} async-done(((bf16[8,256,256]{2,1,0:T(8,128)(2,1)}), bf16[2,256,256]{2,1,0:T(8,128)(2,1)}) %reduce-scatter.2.cloned.1.call-update) | async-done | bytes 262160 | tf_op jit(solution)/shard_map/reduce_scatter | solution.py:37
  42.2 1.0 %convert_multiply_fusion = f32[2,256,256]{2,1,0:T(8,128)S(1)} fusion(bf16[2,256,256]{2,1,0:T(8,128)(2,1)} %reduce-scatter.2.cloned.1.call-done), kind=kLoop, calls=%fused_computation.43 | loop fusion | flops 262144 | bytes 786432 | tf_op jit(solution)/shard_map/div | solution.py:37
  43.1 0.0 copy-start.1
  43.2 0.0 copy-done.2
  43.2 0.0 copy-done.3
  43.2 0.7 copy-done.1
  44.0 0.7 pad_maximum_fusion
  44.7 0.0 all-gather.2.cloned.1.call-update
  44.7 41.3 %all-gather.2.cloned.1.call-done = bf16[8,256,256]{2,1,0:T(8,128)(2,1)} async-done(((bf16[2,256,256]{2,1,0:T(8,128)(2,1)}), bf16[8,256,256]{2,1,0:T(8,128)(2,1)}) %all-gather.2.cloned.1.call-update) | async-done | bytes 1048592 | tf_op jit(solution)/shard_map/all_gather | solution.py:61
  86.1 0.0 copy-done
  86.1 1.8 %fusion.20 = bf16[256,8,256]{0,2,1:T(8,128)(2,1)S(1)} fusion(bf16[8,256,256]{2,1,0:T(8,128)(2,1)} %all-gather.2.cloned.1.call-done, bf16[256,8,256]{2,1,0:T(8,128)(2,1)S(1)} %copy-done), kind=kOutput, calls=%fused_computation.40 | convolution fusion | flops 268959744 | bytes 3145728 | tf_op jit(solution)/shard_map/rkb,kbc->rkc/dot_general | solution.py:58
  87.8 1.8 %copy.19 = bf16[256,8,256]{2,1,0:T(8,128)(2,1)} copy(bf16[256,8,256]{0,2,1:T(8,128)(2,1)S(1)} %fusion.20) | data formatting | bytes 2097152
  (4 shorter events, 0.1 us)
Async XLA Ops:
  7.2 78.9 %copy-start = (bf16[256,8,256]{2,1,0:T(8,128)(2,1)S(1)}, bf16[256,8,256]{2,1,0:T(8,128)(2,1)}, u32[]{:S(2)}) copy-start(bf16[256,8,256]{2,1,0:T(8,128)(2,1)} %param.13) | copy-start | bytes 3145732
  7.2 35.0 %reduce-scatter.2.cloned.1.call-start = ((), (), s32[]{:S(2)}) async-start(), calls=%async_computation.1 | async-start | bytes 1310720 | tf_op jit(solution)/shard_map/reduce_scatter | solution.py:37
  10.5 0.7 copy-start.4
  10.5 32.7 %copy-start.2 = (bf16[2,256,256]{2,1,0:T(8,128)(2,1)S(1)}, bf16[2,256,256]{2,1,0:T(8,128)(2,1)}, u32[]{:S(2)}) copy-start(bf16[2,256,256]{2,1,0:T(8,128)(2,1)} %param.12) | copy-start | bytes 786436
  10.5 32.7 %copy-start.3 = (f32[2]{0:T(128)S(1)}, f32[2]{0:T(128)}, u32[]{:S(2)}) copy-start(f32[2]{0:T(128)} %param.11) | copy-start | bytes 28
  10.5 75.6 %all-gather.2.cloned.1.call-start = ((), (), s32[]{:S(2)}) async-start(), calls=%async_computation.2 | async-start | bytes 1310720 | tf_op jit(solution)/shard_map/all_gather | solution.py:61
  43.1 0.8 copy-start.1
Sparse Core Ops, SparseCore 0:
  11.5 30.6 reduce-scatter.1
  44.8 41.1 all-gather.1
where the time goes:
time: 96.7 us; the launch traced here: 96.5 us
  waiting for transfers between devices  70.5 us (73%)
  between operations  15.4 us (16%)
  matrix products  5 us (5%)
  local copies, waits for them, and re-layouts  3.71 us (4%)
  other arithmetic  1.72 us (2%)
    all_gather x1, waiting for transfers between devices, local(): lax.all_gather(new_inverse, 'rep', axis=0, tiled=True)  41.3 us
    reduce_scatter x1, waiting for transfers between devices, local(): lax.psum_scatter(jnp.einsum('tkb,tkc->kbc', acts, acts, preferred_element...  29.2 us
    dot_general x1, matrix products, local(): jnp.einsum('tkb,tkc->kbc', acts, acts, preferred_element_type=jnp.float32)  3.23 us
    unnamed x11, local copies, waits for them, and re-layouts  3.11 us
  transfers between devices with their start and end apart: 2, of which 2 were waited for; matrix products, arithmetic and copies ran while one was open for 1% of the time, Pallas kernels for 0%

commit v1 on v0

v1 whole, which is shorter than its diff:
```python
import functools

import jax
import jax.numpy as jnp
from jax import lax
from jax.experimental import pallas as pl
from jax.experimental.pallas import tpu as pltpu
from jax.sharding import PartitionSpec as P

ITERS = 5
MESH = pl.DeviceIdType.MESH
F32 = jnp.float32
BF16 = jnp.bfloat16


def split(x):
    high = x.astype(BF16)
    return high, (x - high.astype(F32)).astype(BF16)


def dot3(lhs, rhs):
    lh, ll = lhs
    rh, rl = rhs
    mm = functools.partial(jnp.dot, preferred_element_type=F32)
    return mm(lh, rh) + (mm(lh, rl) + mm(ll, rh))


def partner(me, step, n):
    if n & (n - 1):
        return lax.rem(me + step, n), lax.rem(me + n - step, n)
    other = me
    bit = 1
    while bit < n:
        if step & bit:
            other = other + bit * (1 - 2 * lax.rem(me // bit, 2))
        bit *= 2
    return other, other


def kernel(
    n,
    held,
    groups,
    tokens_all,
    acts_hbm,
    refresh_ref,
    damping_ref,
    old_hbm,
    grads_hbm,
    cov_ref,
    inv_ref,
    pre_ref,
    acts_v,
    grads_v,
    old_v,
    acts_f,
    grads_f,
    pre_f,
    own_f,
    out_buf,
    in_buf,
    gathered,
    load_sem,
    rs_send,
    rs_recv,
    ag_send,
    ag_recv,
):
    me = lax.axis_index("rep")
    blocks = n * held
    order = inv_ref.shape[-1]
    half = order // 2
    rows = acts_v.shape[0] // blocks
    relay = n == 4
    halves = order // 2

    barrier = pltpu.get_barrier_semaphore()
    for step in range(1, n):
        pl.semaphore_signal(
            barrier, inc=1, device_id={"rep": partner(me, step, n)[0]}, device_id_type=MESH
        )

    loads = [
        pltpu.make_async_copy(acts_hbm, acts_v, load_sem.at[0]),
        pltpu.make_async_copy(grads_hbm, grads_v, load_sem.at[1]),
        pltpu.make_async_copy(old_hbm, old_v, load_sem.at[2]),
    ]
    for load in loads:
        load.start()

    row_id = lax.broadcasted_iota(jnp.int32, (half, half), 0)
    col_id = lax.broadcasted_iota(jnp.int32, (half, half), 1)
    upper = col_id >= row_id
    on_diag = col_id == row_id

    def widen(source, target):
        for tile in range(order // 128):
            target[tile] = source[:, tile * 128 : (tile + 1) * 128].astype(F32)

    def take(source, block):
        return jnp.concatenate(
            [
                source[tile, pl.ds(block, rows, stride=blocks), :]
                for tile in range(order // 128)
            ],
            axis=1,
        ).astype(BF16)

    def gram(block):
        part = take(acts_f, block)
        full = lax.dot_general(
            part, part, (((0,), (0,)), ((), ())), preferred_element_type=F32
        )
        low = full[half:, half:]
        last = jnp.sum(jnp.where(on_diag, low, 0.0), axis=0, keepdims=True)
        return full[:half, half:], jnp.where(upper, full[:half, :half], low), last

    loads[0].wait()
    widen(acts_v, acts_f)

    rs = {}
    greeted = False
    steps = list(range(n - 1, 0, -1))
    for slot in range(held):
        for step in steps:
            target = partner(me, step, n)[0]
            cross, packed, last = gram(target * held + slot)
            place = out_buf.at[step - 1, slot]
            place[:half, :] = cross.astype(BF16)
            place[half : 2 * half, :] = packed.astype(BF16)
            place[2 * half :, :] = jnp.broadcast_to(last, (16, half)).astype(BF16)
            if not greeted:
                pl.semaphore_wait(barrier, n - 1)
                greeted = True
            copy = pltpu.make_async_remote_copy(
                src_ref=place,
                dst_ref=in_buf.at[step - 1, slot],
                send_sem=rs_send.at[step - 1, slot],
                recv_sem=rs_recv.at[step - 1, slot],
                device_id={"rep": target},
                device_id_type=MESH,
            )
            copy.start()
            rs[step, slot] = copy
        cross, packed, last = gram(me * held + slot)
        own_f[slot, :half, :] = cross
        own_f[slot, half : 2 * half, :] = packed
        own_f[slot, 2 * half :, :] = jnp.broadcast_to(last, (8, half))

    loads[1].wait()
    widen(grads_v, grads_f)
    loads[2].wait()

    eye = jnp.where(
        lax.broadcasted_iota(jnp.int32, (order, order), 0)
        == lax.broadcasted_iota(jnp.int32, (order, order), 1),
        1.0,
        0.0,
    ).astype(F32)

    ag = {}

    def ship(key, source, target, step, sem):
        copy = pltpu.make_async_remote_copy(
            src_ref=source,
            dst_ref=target,
            send_sem=ag_send.at[sem],
            recv_sem=ag_recv.at[sem],
            device_id={"rep": partner(me, step, n)[0]},
            device_id_type=MESH,
        )
        copy.start()
        ag[key] = copy

    def refresh_block(slot):
        total = own_f[slot]
        total_cross, total_packed, total_last = (
            total[:half],
            total[half : 2 * half],
            total[2 * half : 2 * half + 1],
        )
        for step in steps:
            rs[step, slot].wait_recv()
            came = in_buf[step - 1, slot].astype(F32)
            total_cross = total_cross + came[:half]
            total_packed = total_packed + came[half : 2 * half]
            total_last = total_last + came[2 * half : 2 * half + 1]
        scale = 1.0 / tokens_all
        flipped = total_packed.T
        first = jnp.where(upper, total_packed, flipped)
        second = jnp.where(
            on_diag,
            jnp.broadcast_to(total_last, (half, half)),
            jnp.where(upper, flipped, total_packed),
        )
        covariance = (
            jnp.concatenate(
                [
                    jnp.concatenate([first, total_cross], axis=1),
                    jnp.concatenate([total_cross.T, second], axis=1),
                ],
                axis=0,
            )
            * scale
        )
        cov_ref[slot] = covariance
        matrix = covariance + damping_ref[slot] * eye
        bound = jnp.max(jnp.sum(jnp.abs(matrix), axis=0, keepdims=True), axis=1, keepdims=True)
        inverse_bound = 1.0 / bound
        residual = eye - matrix * inverse_bound
        series = eye + residual
        power = split(residual)
        power = split(dot3(power, power))
        for iteration in range(2, ITERS):
            left = split(series)
            square = dot3(power, power)
            series = series + dot3(left, power)
            power = split(square)
        series = series + dot3(split(series), power)
        approx = (series * inverse_bound).astype(BF16)
        due = jnp.full((order, order), refresh_ref[slot], jnp.int32) != groups
        chosen = jnp.where(due, approx, old_v[slot])
        inv_ref[slot] = chosen
        gathered[0, slot] = chosen
        if relay:
            top, bottom = pl.ds(0, halves), pl.ds(halves, halves)
            for part, (step, piece) in enumerate(((1, top), (2, bottom), (1, bottom), (2, top))):
                ship(
                    (slot, part),
                    gathered.at[0, slot, piece],
                    gathered.at[step, slot, piece],
                    step,
                    slot * 6 + part,
                )
        else:
            for step in steps:
                ship(
                    (slot, step),
                    gathered.at[0, slot],
                    gathered.at[step, slot],
                    step,
                    slot * 6 * n + step,
                )

    def forward(slot):
        top, bottom = pl.ds(0, halves), pl.ds(halves, halves)
        ag[slot, 0].wait_recv()
        ship((slot, 4), gathered.at[1, slot, top], gathered.at[3, slot, top], 2, slot * 6 + 4)
        ag[slot, 1].wait_recv()
        ship((slot, 5), gathered.at[2, slot, bottom], gathered.at[3, slot, bottom], 1, slot * 6 + 5)

    def apply(step, slot):
        block = partner(me, step, n)[1] * held + slot
        result = jnp.dot(
            take(grads_f, block), gathered[step, slot], preferred_element_type=F32
        )
        for tile in range(order // 128):
            pre_f[tile, pl.ds(block, rows, stride=blocks), :] = result[
                :, tile * 128 : (tile + 1) * 128
            ]

    for slot in range(held):
        refresh_block(slot)
        if relay and slot > 0:
            forward(slot - 1)
    if relay:
        forward(held - 1)
    for slot in range(held):
        apply(0, slot)
    for slot in range(held):
        if relay:
            ag[slot, 2].wait_recv()
            apply(1, slot)
            ag[slot, 3].wait_recv()
            apply(2, slot)
            ag[slot, 4].wait_recv()
            ag[slot, 5].wait_recv()
            apply(3, slot)
        else:
            for step in steps:
                ag[slot, step].wait_recv()
                apply(step, slot)
    for tile in range(order // 128):
        pre_ref[:, tile * 128 : (tile + 1) * 128] = pre_f[tile].astype(BF16)
    for copy in rs.values():
        copy.wait_send()
    for copy in ag.values():
        copy.wait_send()


def local(acts, refresh, damping, old_inverse, grads):
    n = lax.axis_size("rep")
    groups = lax.axis_size("mp")
    rows, blocks, order = acts.shape
    grad_rows = grads.shape[0]
    held = refresh.shape[0]
    half = order // 2
    tiles = order // 128
    copies = held * 6 if n == 4 else held * 6 * n
    any_space = pl.BlockSpec(memory_space=pl.ANY)
    smem = pl.BlockSpec(memory_space=pltpu.SMEM)
    vmem = pl.BlockSpec(memory_space=pltpu.VMEM)
    covariance, new_inverse, precond = pl.pallas_call(
        functools.partial(kernel, n, held, groups, rows * n),
        out_shape=(
            jax.ShapeDtypeStruct((held, order, order), F32),
            jax.ShapeDtypeStruct((held, order, order), BF16),
            jax.ShapeDtypeStruct((grad_rows * blocks, order), BF16),
        ),
        in_specs=[any_space, smem, smem, any_space, any_space],
        out_specs=(vmem, vmem, vmem),
        scratch_shapes=[
            pltpu.VMEM((rows * blocks, order), BF16),
            pltpu.VMEM((grad_rows * blocks, order), BF16),
            pltpu.VMEM((held, order, order), BF16),
            pltpu.VMEM((tiles, rows * blocks, 128), F32),
            pltpu.VMEM((tiles, grad_rows * blocks, 128), F32),
            pltpu.VMEM((tiles, grad_rows * blocks, 128), F32),
            pltpu.VMEM((held, order + 8, half), F32),
            pltpu.VMEM((n - 1, held, order + 16, half), BF16),
            pltpu.VMEM((n - 1, held, order + 16, half), BF16),
            pltpu.VMEM((n, held, order, order), BF16),
            pltpu.SemaphoreType.DMA((3,)),
            pltpu.SemaphoreType.DMA((n - 1, held)),
            pltpu.SemaphoreType.DMA((n - 1, held)),
            pltpu.SemaphoreType.DMA((copies,)),
            pltpu.SemaphoreType.DMA((copies,)),
        ],
        compiler_params=pltpu.CompilerParams(
            collective_id=0, has_side_effects=True, vmem_limit_bytes=63 << 20
        ),
    )(
        acts.reshape(rows * blocks, order),
        refresh,
        damping,
        old_inverse,
        grads.reshape(grad_rows * blocks, order),
    )
    return covariance, new_inverse, precond.reshape(grad_rows, blocks, order)


def solution(mesh):
    return jax.shard_map(
        local,
        mesh=mesh,
        in_specs=(
            P("rep", "mp", None),
            P(("mp", "rep")),
            P(("mp", "rep")),
            P(("mp", "rep"), None, None),
            P("rep", "mp", None),
        ),
        out_specs=(
            P(("mp", "rep"), None, None),
            P(("mp", "rep"), None, None),
            P("rep", "mp", None),
        ),
        check_vma=False,
    )
```

time: 96.7 us -> 29.9 us (0.31)
  waiting for transfers between devices: 70.5 us -> 0 us
  Pallas kernels: 0 us -> 24.5 us
  between operations: 15.4 us -> 0.65 us
  matrix products: 5 us -> 0 us
  other arithmetic: 1.72 us -> 0 us
    all_gather x1 -> x0, waiting for transfers between devices: 41.3 us -> none  [local(): lax.all_gather(new_inverse, 'rep', axis=0, tiled=True)]
    reduce_scatter x1 -> x0, waiting for transfers between devices: 29.2 us -> none  [local(): lax.psum_scatter(jnp.einsum('tkb,tkc->kbc', acts, acts, preferred_element...]
    pallas_call x0 -> x1, Pallas kernels: none -> 24.5 us  [local(): pl.pallas_call(functools.partial(kernel, n, held, groups, rows * n), out_...]
    dot_general x2 -> x0, matrix products: 5 us -> none  [the longest x1 3.23 us: local(): jnp.einsum('tkb,tkc->kbc', acts, acts, preferred_element_type=jnp.float32)]
    unnamed x11 -> x5, local copies, waits for them, and re-layouts: 3.11 us -> 4.6 us
    div x1 -> x0, other arithmetic: 0.99 us -> none  [local(): lax.psum_scatter(jnp.einsum('tkb,tkc->kbc', acts, acts, preferred_element...]
  transfers between devices with their start and end apart: 2 -> 0, of which waited for: 2 -> 0; matrix products, arithmetic and copies ran while one was open for 1% -> 0% of each run, Pallas kernels for 0% -> 0%
where the time goes in v1:
time: 29.9 us; the launch traced here: 29.7 us
  Pallas kernels  24.5 us (82%)
  local copies, waits for them, and re-layouts  4.6 us (15%)
  between operations  0.65 us (2%)
    pallas_call x1, Pallas kernels, local(): pl.pallas_call(functools.partial(kernel, n, held, groups, rows * n), out_...  24.5 us
    unnamed x5, local copies, waits for them, and re-layouts  4.6 us

profile of v1, /device:TPU:0, one launch (start us, length us, event | category | flops | bytes accessed | tf_op | source)
XLA Modules:
  0.0 29.7 jit_solution(18106198412699870838)
XLA Ops:
  0.6 24.5 %shard_map.76 = (f32[2,256,256]{2,1,0:T(8,128)}, bf16[2,256,256]{2,1,0:T(8,128)(2,1)}, bf16[2048,256]{1,0:T(8,128)(2,1)}) custom-call(bf16[2048,256]{1,0:T(8,128)(2,1)} %bitcast.3, s32[2]{0:T(128)} %refresh_ref.1, f32[2]{0:T(128)} %damping_ref.1, bf16[2,256,256]{2,1,0:T(8,128)(2,1)} %old_hbm.1, bf16[2048,256]{1,0:T(8,128)(2,1)} %bitcast.4), custom_call_target="tpu_custom_call" | custom-call | tf_op jit(solution)/shard_map/pallas_call | solution.py:303
  25.1 0.0 copy-start
  25.1 2.0 %copy.11 = f32[2,256,256]{2,1,0:T(8,128)} copy(f32[2,256,256]{2,1,0:T(8,128)} %get-tuple-element.12) | data formatting | bytes 1048576
  27.1 1.7 %copy.12 = bf16[2,256,256]{2,1,0:T(8,128)(2,1)} copy(bf16[2,256,256]{2,1,0:T(8,128)(2,1)} %get-tuple-element.13) | data formatting | bytes 524288
  28.8 0.0 copy-done
  28.8 1.0 %copy.13 = bf16[256,8,256]{2,1,0:T(8,128)(2,1)} copy(bf16[256,8,256]{2,1,0:T(8,128)(2,1)S(1)} %bitcast.5) | data formatting | bytes 2097152
Async XLA Ops:
  25.1 3.6 %copy-start = (bf16[2048,256]{1,0:T(8,128)(2,1)S(1)}, bf16[2048,256]{1,0:T(8,128)(2,1)}, u32[]{:S(2)}) copy-start(bf16[2048,256]{1,0:T(8,128)(2,1)} %get-tuple-element.8) | copy-start | bytes 3145732

commit v2 on v1

--- a/solution.py
+++ b/solution.py
@@ -1,4 +1,5 @@
 import functools
+import math
 
 import jax
 import jax.numpy as jnp
@@ -8,6 +9,7 @@
 from jax.sharding import PartitionSpec as P
 
 ITERS = 5
+CHUNKS = 4
 MESH = pl.DeviceIdType.MESH
 F32 = jnp.float32
 BF16 = jnp.bfloat16
@@ -49,13 +51,12 @@
     grads_hbm,
     cov_ref,
     inv_ref,
-    pre_ref,
+    pre_f,
     acts_v,
     grads_v,
     old_v,
     acts_f,
     grads_f,
-    pre_f,
     own_f,
     out_buf,
     in_buf,
@@ -280,12 +281,29 @@
             for step in steps:
                 ag[slot, step].wait_recv()
                 apply(step, slot)
-    for tile in range(order // 128):
-        pre_ref[:, tile * 128 : (tile + 1) * 128] = pre_f[tile].astype(BF16)
     for copy in rs.values():
         copy.wait_send()
     for copy in ag.values():
         copy.wait_send()
+
+
+def deliver(cov_v, inv_v, wide, cov_hbm, inv_hbm, pre_hbm, narrow, sem):
+    copies = [
+        pltpu.make_async_copy(cov_v, cov_hbm, sem.at[0]),
+        pltpu.make_async_copy(inv_v, inv_hbm, sem.at[1]),
+    ]
+    for copy in copies:
+        copy.start()
+    size = narrow.shape[0] // CHUNKS
+    for chunk in range(CHUNKS):
+        part = pl.ds(chunk * size, size)
+        for tile in range(wide.shape[0]):
+            narrow[part, tile * 128 : (tile + 1) * 128] = wide[tile, part, :].astype(BF16)
+        copy = pltpu.make_async_copy(narrow.at[part], pre_hbm.at[part], sem.at[2 + chunk])
+        copy.start()
+        copies.append(copy)
+    for copy in copies:
+        copy.wait()
 
 
 def local(acts, refresh, damping, old_inverse, grads):
@@ -297,45 +315,67 @@
     half = order // 2
     tiles = order // 128
     copies = held * 6 if n == 4 else held * 6 * n
-    any_space = pl.BlockSpec(memory_space=pl.ANY)
+    any_space = pl.BlockSpec(memory_space=pltpu.HBM)
     smem = pl.BlockSpec(memory_space=pltpu.SMEM)
     vmem = pl.BlockSpec(memory_space=pltpu.VMEM)
+    scratch = [
+        pltpu.VMEM((rows * blocks, order), BF16),
+        pltpu.VMEM((grad_rows * blocks, order), BF16),
+        pltpu.VMEM((held, order, order), BF16),
+        pltpu.VMEM((tiles, rows * blocks, 128), F32),
+        pltpu.VMEM((tiles, grad_rows * blocks, 128), F32),
+        pltpu.VMEM((held, order + 8, half), F32),
+        pltpu.VMEM((n - 1, held, order + 16, half), BF16),
+        pltpu.VMEM((n - 1, held, order + 16, half), BF16),
+        pltpu.VMEM((n, held, order, order), BF16),
+        pltpu.SemaphoreType.DMA((3,)),
+        pltpu.SemaphoreType.DMA((n - 1, held)),
+        pltpu.SemaphoreType.DMA((n - 1, held)),
+        pltpu.SemaphoreType.DMA((copies,)),
+        pltpu.SemaphoreType.DMA((copies,)),
+        ]
+    need = sum(
+        math.prod(item.shape) * jnp.dtype(item.dtype).itemsize
+        for item in scratch
+        if item.memory_space == pltpu.VMEM
+    )
+    covariance, new_inverse, wide = pl.pallas_call(
+        functools.partial(kernel, n, held, groups, rows * n),
+        out_shape=(
+            pltpu.VMEM((held, order, order), F32),
+            pltpu.VMEM((held, order, order), BF16),
+            pltpu.VMEM((tiles, grad_rows * blocks, 128), F32),
+        ),
+        in_specs=[any_space, smem, smem, any_space, any_space],
+        out_specs=(vmem, vmem, vmem),
+        scratch_shapes=scratch,
+        compiler_params=pltpu.CompilerParams(
+            collective_id=0, has_side_effects=True, vmem_limit_bytes=need + (8 << 20)
+        ),
+    )(
+        pltpu.with_memory_space_constraint(acts.reshape(rows * blocks, order), pltpu.HBM),
+        pltpu.with_memory_space_constraint(refresh, pltpu.HBM),
+        pltpu.with_memory_space_constraint(damping, pltpu.HBM),
+        pltpu.with_memory_space_constraint(old_inverse, pltpu.HBM),
+        pltpu.with_memory_space_constraint(grads.reshape(grad_rows * blocks, order), pltpu.HBM),
+    )
     covariance, new_inverse, precond = pl.pallas_call(
-        functools.partial(kernel, n, held, groups, rows * n),
+        deliver,
         out_shape=(
             jax.ShapeDtypeStruct((held, order, order), F32),
             jax.ShapeDtypeStruct((held, order, order), BF16),
             jax.ShapeDtypeStruct((grad_rows * blocks, order), BF16),
         ),
-        in_specs=[any_space, smem, smem, any_space, any_space],
-        out_specs=(vmem, vmem, vmem),
+        in_specs=[vmem] * 3,
+        out_specs=(any_space,) * 3,
         scratch_shapes=[
-            pltpu.VMEM((rows * blocks, order), BF16),
             pltpu.VMEM((grad_rows * blocks, order), BF16),
-            pltpu.VMEM((held, order, order), BF16),
-            pltpu.VMEM((tiles, rows * blocks, 128), F32),
-            pltpu.VMEM((tiles, grad_rows * blocks, 128), F32),
-            pltpu.VMEM((tiles, grad_rows * blocks, 128), F32),
-            pltpu.VMEM((held, order + 8, half), F32),
-            pltpu.VMEM((n - 1, held, order + 16, half), BF16),
-            pltpu.VMEM((n - 1, held, order + 16, half), BF16),
-            pltpu.VMEM((n, held, order, order), BF16),
-            pltpu.SemaphoreType.DMA((3,)),
-            pltpu.SemaphoreType.DMA((n - 1, held)),
-            pltpu.SemaphoreType.DMA((n - 1, held)),
-            pltpu.SemaphoreType.DMA((copies,)),
-            pltpu.SemaphoreType.DMA((copies,)),
+            pltpu.SemaphoreType.DMA((2 + CHUNKS,)),
         ],
         compiler_params=pltpu.CompilerParams(
-            collective_id=0, has_side_effects=True, vmem_limit_bytes=63 << 20
-        ),
-    )(
-        acts.reshape(rows * blocks, order),
-        refresh,
-        damping,
-        old_inverse,
-        grads.reshape(grad_rows * blocks, order),
-    )
+            vmem_limit_bytes=grad_rows * blocks * order * 2 + (2 << 20)
+        ),
+    )(covariance, new_inverse, wide)
     return covariance, new_inverse, precond.reshape(grad_rows, blocks, order)
 
 

time: 29.9 us -> 25.2 us (0.84)
  local copies, waits for them, and re-layouts: 4.6 us -> 0 us
    unnamed x5 -> x0, local copies, waits for them, and re-layouts: 4.6 us -> none
    pallas_call x1, Pallas kernels: 24.5 us -> 23.1 us  [local(): pl.pallas_call(functools.partial(kernel, n, held, groups, rows * n), out_...]
    pallas_call x0 -> x1, Pallas kernels: none -> 1.27 us  [local(): pl.pallas_call(deliver, out_shape=(jax.ShapeDtypeStruct((held, order, ord...]
where the time goes in v2:
time: 25.2 us; the launch traced here: 25 us
  Pallas kernels  24.4 us (97%)
  between operations  0.64 us (3%)
    pallas_call x1, Pallas kernels, local(): pl.pallas_call(functools.partial(kernel, n, held, groups, rows * n), out_...  23.1 us
    pallas_call x1, Pallas kernels, local(): pl.pallas_call(deliver, out_shape=(jax.ShapeDtypeStruct((held, order, ord...  1.27 us

profile of v2, /device:TPU:0, one launch (start us, length us, event | category | flops | bytes accessed | tf_op | source)
XLA Modules:
  0.0 25.0 jit_solution(11990516081845607892)
XLA Ops:
  0.6 23.1 %shard_map.76 = (f32[2,256,256]{2,1,0:T(8,128)S(1)}, bf16[2,256,256]{2,1,0:T(8,128)(2,1)S(1)}, f32[2,2048,128]{2,1,0:T(8,128)S(1)}) custom-call(bf16[2048,256]{1,0:T(8,128)(2,1)} %bitcast.3, s32[2]{0:T(128)} %refresh_ref.1, f32[2]{0:T(128)} %damping_ref.1, bf16[2,256,256]{2,1,0:T(8,128)(2,1)} %old_hbm.1, bf16[2048,256]{1,0:T(8,128)(2,1)} %bitcast.4), custom_call_target="tpu_custom_call" | custom-call | tf_op jit(solution)/shard_map/pallas_call | solution.py:342
  23.7 1.3 %shard_map.77 = (f32[2,256,256]{2,1,0:T(8,128)}, bf16[2,256,256]{2,1,0:T(8,128)(2,1)}, bf16[2048,256]{1,0:T(8,128)(2,1)}) custom-call(f32[2,256,256]{2,1,0:T(8,128)S(1)} %get-tuple-element.9.cov_v, bf16[2,256,256]{2,1,0:T(8,128)(2,1)S(1)} %get-tuple-element.10.inv_v, f32[2,2048,128]{2,1,0:T(8,128)S(1)} %get-tuple-element.11.wide), custom_call_target="tpu_custom_call" | custom-call | tf_op jit(solution)/shard_map/pallas_call | solution.py:362

commit v3 on v2

--- a/solution.py
+++ b/solution.py
@@ -10,6 +10,7 @@
 
 ITERS = 5
 CHUNKS = 4
+LOADS = 4
 MESH = pl.DeviceIdType.MESH
 F32 = jnp.float32
 BF16 = jnp.bfloat16
@@ -81,8 +82,11 @@
             barrier, inc=1, device_id={"rep": partner(me, step, n)[0]}, device_id_type=MESH
         )
 
+    piece = acts_v.shape[0] // LOADS
     loads = [
-        pltpu.make_async_copy(acts_hbm, acts_v, load_sem.at[0]),
+        pltpu.make_async_copy(acts_hbm.at[pl.ds(c * piece, piece)], acts_v.at[pl.ds(c * piece, piece)], load_sem.at[3 + c])
+        for c in range(LOADS)
+    ] + [
         pltpu.make_async_copy(grads_hbm, grads_v, load_sem.at[1]),
         pltpu.make_async_copy(old_hbm, old_v, load_sem.at[2]),
     ]
@@ -116,8 +120,11 @@
         last = jnp.sum(jnp.where(on_diag, low, 0.0), axis=0, keepdims=True)
         return full[:half, half:], jnp.where(upper, full[:half, :half], low), last
 
-    loads[0].wait()
-    widen(acts_v, acts_f)
+    for c in range(LOADS):
+        loads[c].wait()
+        part = pl.ds(c * piece, piece)
+        for tile in range(order // 128):
+            acts_f[tile, part, :] = acts_v[part, tile * 128 : (tile + 1) * 128].astype(F32)
 
     rs = {}
     greeted = False
@@ -148,9 +155,9 @@
         own_f[slot, half : 2 * half, :] = packed
         own_f[slot, 2 * half :, :] = jnp.broadcast_to(last, (8, half))
 
-    loads[1].wait()
+    loads[LOADS].wait()
     widen(grads_v, grads_f)
-    loads[2].wait()
+    loads[LOADS + 1].wait()
 
     eye = jnp.where(
         lax.broadcasted_iota(jnp.int32, (order, order), 0)
@@ -160,6 +167,7 @@
     ).astype(F32)
 
     ag = {}
+    settled = set()
 
     def ship(key, source, target, step, sem):
         copy = pltpu.make_async_remote_copy(
@@ -226,6 +234,11 @@
         if relay:
             top, bottom = pl.ds(0, halves), pl.ds(halves, halves)
             for part, (step, piece) in enumerate(((1, top), (2, bottom), (1, bottom), (2, top))):
+                if part == 2 and slot > 0:
+                    for sent in (0, 1):
+                        ag[slot, sent].wait_send()
+                        settled.add((slot, sent))
+                    forward(slot - 1)
                 ship(
                     (slot, part),
                     gathered.at[0, slot, piece],
@@ -262,8 +275,6 @@
 
     for slot in range(held):
         refresh_block(slot)
-        if relay and slot > 0:
-            forward(slot - 1)
     if relay:
         forward(held - 1)
     for slot in range(held):
@@ -283,8 +294,9 @@
                 apply(step, slot)
     for copy in rs.values():
         copy.wait_send()
-    for copy in ag.values():
-        copy.wait_send()
+    for key, copy in ag.items():
+        if key not in settled:
+            copy.wait_send()
 
 
 def deliver(cov_v, inv_v, wide, cov_hbm, inv_hbm, pre_hbm, narrow, sem):
@@ -328,7 +340,7 @@
         pltpu.VMEM((n - 1, held, order + 16, half), BF16),
         pltpu.VMEM((n - 1, held, order + 16, half), BF16),
         pltpu.VMEM((n, held, order, order), BF16),
-        pltpu.SemaphoreType.DMA((3,)),
+        pltpu.SemaphoreType.DMA((3 + LOADS,)),
         pltpu.SemaphoreType.DMA((n - 1, held)),
         pltpu.SemaphoreType.DMA((n - 1, held)),
         pltpu.SemaphoreType.DMA((copies,)),

time: 25.2 us -> 24.8 us (0.984)
  Pallas kernels: 24.4 us -> 24 us
    pallas_call x1, Pallas kernels: 23.1 us -> 22.7 us  [local(): pl.pallas_call(functools.partial(kernel, n, held, groups, rows * n), out_...]
where the time goes in v3:
time: 24.8 us; the launch traced here: 24.6 us
  Pallas kernels  24 us (97%)
  between operations  0.64 us (3%)
    pallas_call x1, Pallas kernels, local(): pl.pallas_call(functools.partial(kernel, n, held, groups, rows * n), out_...  22.7 us
    pallas_call x1, Pallas kernels, local(): pl.pallas_call(deliver, out_shape=(jax.ShapeDtypeStruct((held, order, ord...  1.27 us

profile of v3, /device:TPU:0, one launch (start us, length us, event | category | flops | bytes accessed | tf_op | source)
XLA Modules:
  0.0 24.6 jit_solution(3562618495786860888)
XLA Ops:
  0.6 22.7 %shard_map.76 = (f32[2,256,256]{2,1,0:T(8,128)S(1)}, bf16[2,256,256]{2,1,0:T(8,128)(2,1)S(1)}, f32[2,2048,128]{2,1,0:T(8,128)S(1)}) custom-call(bf16[2048,256]{1,0:T(8,128)(2,1)} %bitcast.3, s32[2]{0:T(128)} %refresh_ref.1, f32[2]{0:T(128)} %damping_ref.1, bf16[2,256,256]{2,1,0:T(8,128)(2,1)} %old_hbm.1, bf16[2048,256]{1,0:T(8,128)(2,1)} %bitcast.4), custom_call_target="tpu_custom_call" | custom-call | tf_op jit(solution)/shard_map/pallas_call | solution.py:354
  23.3 1.3 %shard_map.77 = (f32[2,256,256]{2,1,0:T(8,128)}, bf16[2,256,256]{2,1,0:T(8,128)(2,1)}, bf16[2048,256]{1,0:T(8,128)(2,1)}) custom-call(f32[2,256,256]{2,1,0:T(8,128)S(1)} %get-tuple-element.9.cov_v, bf16[2,256,256]{2,1,0:T(8,128)(2,1)S(1)} %get-tuple-element.10.inv_v, f32[2,2048,128]{2,1,0:T(8,128)S(1)} %get-tuple-element.11.wide), custom_call_target="tpu_custom_call" | custom-call | tf_op jit(solution)/shard_map/pallas_call | solution.py:374
